TPU v7x, 32 devices: a whole 2x2x4 slice. The times are simulated.
32 devices in a mesh: groups: 2 (over y), sec: 2 (over x), row: 4 (over z), col: 2 (over core).
Axes of the slice: x: 2, y: 2, z: 4, core: 2. Of those that a mesh axis runs over, the one named last changes fastest.
Arguments:
- factors: bfloat16 [4, 2048, 2048], P(('groups', 'sec'), 'row', 'col'), parts along dimension 0, may hold values from -0.125 to 0.125
- inverses: bfloat16 [4, 2048, 2048], P(('groups', 'sec'), 'row', 'col'), parts along dimension 0, may hold values from -1.4 to 1.4, as said below
- sigma_end: float32 [4096, 2048], P(('groups', 'row'), 'col'), parts along dimension 0, may hold values from -1 to 6, as said below
Outputs:
- variance: float32 [4, 2048, 2048], P(('groups', 'sec'), 'row', 'col'), parts along dimension 0
There are 2 independent parts, one for each index of `groups`. A program takes and returns all parts, laid end to end along the dimension named above; each array names one. Nothing has to cross between parts.
Inputs may be any that keep to these rules, and one draw needn't show every extreme that they name: inverses[t] is lower triangular; its diagonal entries lie in 0.6 to 1.4. sigma_end is symmetric with diagonal entries in 2.5 to 6.
All inputs are finite; a program needn't handle non-finite values.
Results may differ from a plain program's by a relative error of at most 0.011.
Values may be sent and summed in bfloat16 or wider, within the bound.
A program may use at most 64 MiB of HBM per device.

v0:
```python
import jax
import jax.numpy as jnp
from jax import lax
from jax.sharding import PartitionSpec as P


def partner(shard, axis, stride):
    return lax.ppermute(shard, axis, [(i, i ^ 1 << stride) for i in range(lax.axis_size(axis))])


def passed_along(value, axis, steps):
    count = lax.axis_size(axis)
    first, last = (max(0, -steps), min(count, count - steps))
    return lax.ppermute(value, axis, [(source, source + steps) for source in range(first, last)])


def local(factors, inverses, sigma_end):
    row_size = lax.axis_size("row")
    col_size = lax.axis_size("col")
    sec_size = lax.axis_size("sec")
    row_index = lax.axis_index("row")
    col_index = lax.axis_index("col")
    sec_index = lax.axis_index("sec")
    _, tile_rows, _ = factors.shape
    per_column = row_size // col_size
    offset = row_index % per_column * tile_rows
    owns_panel = col_index == row_index // per_column

    def gather(tile):
        return lax.all_gather(tile, "row", axis=0, tiled=True)

    def left_of(full):
        mine = lax.dynamic_slice_in_dim(full, offset, tile_rows, 1)
        return jnp.where(owns_panel, mine, partner(mine, "col", 0))

    def cross(left, full):
        return lax.dot_general(
            left, full, (((0,), (0,)), ((), ())), preferred_element_type=jnp.float32
        )

    current = sigma_end.astype(jnp.bfloat16)
    factor = gather(factors[0])
    state = gather(current)
    inverse = gather(inverses[0])
    factor_left = left_of(factor)
    diagonal = cross(left_of(inverse), inverse)
    result = None
    for segment in range(sec_size):
        half = cross(factor_left, state).astype(jnp.bfloat16)
        whole = lax.all_gather(half, "col", axis=1, tiled=True)
        block = diagonal + jnp.dot(whole, factor, preferred_element_type=jnp.float32)
        active = sec_index == sec_size - 1 - segment
        result = block if result is None else jnp.where(active, block, result)
        if segment < sec_size - 1:
            state = gather(passed_along(block.astype(jnp.bfloat16), "sec", -1))
    return result[None]


def solution(mesh):
    in_specs = (
        P(("groups", "sec"), "row", "col"),
        P(("groups", "sec"), "row", "col"),
        P(("groups", "row"), "col"),
    )
    out_specs = P(("groups", "sec"), "row", "col")
    return jax.shard_map(local, mesh=mesh, in_specs=in_specs, out_specs=out_specs, check_vma=False)
```

profile of v0, /device:TPU:0, one launch (start us, length us, event | category | flops | bytes accessed | tf_op | source)
XLA Modules:
  0.0 415.6 jit_solution(8728628893357089546)
XLA Ops:
  6.5 0.0 all-gather.19.cloned.1.call-start
  6.5 0.7 all-gather.19.cloned.1.call-update
  7.3 0.0 all-gather.17.cloned.1.call-start
  7.3 0.7 all-gather.17.cloned.1.call-update
  8.0 0.0 all-gather.9.cloned.1.call-start
  8.1 2.8 convert_element_type.12
  10.8 0.0 all-gather.9.cloned.1.call-update
  10.8 0.0 all-gather.11.cloned.1.call-start
  10.9 81.5 %all-gather.19.cloned.1.call-done = bf16[1,2048,1024]{2,1,0:T(8,128)(2,1)} async-done(((bf16[1,512,1024]{2,1,0:T(8,128)(2,1)}), bf16[1,2048,1024]{2,1,0:T(8,128)(2,1)}) %all-gather.19.cloned.1.call-update) | async-done | bytes 4194320 | tf_op jit(solution)/shard_map/all_gather | solution.py:30
  92.4 1.7 dynamic-slice_bitcast_fusion
  94.2 0.1 collective-permute-start.1
  94.3 79.1 %all-gather.17.cloned.1.call-done = bf16[1,2048,1024]{2,1,0:T(8,128)(2,1)} async-done(((bf16[1,512,1024]{2,1,0:T(8,128)(2,1)}), bf16[1,2048,1024]{2,1,0:T(8,128)(2,1)}) %all-gather.17.cloned.1.call-update) | async-done | bytes 4194320 | tf_op jit(solution)/shard_map/all_gather | solution.py:30
  173.3 3.0 dynamic-slice_bitcast_fusion.1
  176.4 0.0 collective-permute-start
  176.4 77.9 %all-gather.9.cloned.1.call-done = bf16[2048,1024]{1,0:T(8,128)(2,1)} async-done(((bf16[512,1024]{1,0:T(8,128)(2,1)}), bf16[2048,1024]{1,0:T(8,128)(2,1)}) %all-gather.9.cloned.1.call-update) | async-done | bytes 4194320 | tf_op jit(solution)/shard_map/all_gather | solution.py:30
  254.2 0.0 collective-permute-done.1
  254.2 5.6 %convolution_convert_fusion.1 = bf16[512,1024]{1,0:T(8,128)(2,1)} fusion(bf16[2048,1024]{1,0:T(8,128)(2,1)} %all-gather.9.cloned.1.call-done, bf16[2048,512]{1,0:T(8,128)(2,1)S(1)} %dynamic-slice_bitcast_fusion, bf16[2048,512]{1,0:T(8,128)(2,1)} %collective-permute-done.1, pred[]{:T(512)S(6)} %eq.9), kind=kOutput, calls=%fused_computation.14 | convolution fusion | flops 2149056512 | bytes 9437185 | tf_op jit(solution)/shard_map/dot_general | solution.py:37
  259.8 0.0 all-gather.11.cloned.1.call-update
  259.8 0.0 all-gather.13.cloned.1.call-start
  259.8 0.0 collective-permute-done
  259.9 6.6 %fusion.4 = f32[512,1024]{1,0:T(8,128)} fusion(bf16[1,2048,1024]{2,1,0:T(8,128)(2,1)} %all-gather.17.cloned.1.call-done, bf16[2048,512]{1,0:T(8,128)(2,1)} %dynamic-slice_bitcast_fusion.1, bf16[2048,512]{1,0:T(8,128)(2,1)} %collective-permute-done, pred[]{:T(512)S(6)} %eq.9), kind=kOutput, calls=%fused_computation.4 | convolution fusion | flops 2148532224 | bytes 10485761 | tf_op jit(solution)/shard_map/dot_general | solution.py:37
  266.4 3.2 all-gather.11.cloned.1.call-done
  269.7 7.1 %fusion.13 = (bf16[512,1024]{1,0:T(8,128)(2,1)S(1)}, f32[512,1024]{1,0:T(8,128)}) fusion(f32[512,1024]{1,0:T(8,128)} %fusion.4, bf16[512,2048]{1,0:T(8,128)(2,1)} %all-gather.11.cloned.1.call-done, bf16[1,2048,1024]{2,1,0:T(8,128)(2,1)} %all-gather.19.cloned.1.call-done), kind=kOutput, calls=%fused_computation.15 | convolution fusion | flops 2148532224 | bytes 11534336 | tf_op jit(solution)/shard_map/dot_general | solution.py:51
  276.8 1.3 collective-permute-start.2
  278.1 25.9 %collective-permute-done.2 = bf16[512,1024]{1,0:T(8,128)(2,1)S(1)} collective-permute-done((bf16[512,1024]{1,0:T(8,128)(2,1)S(1)}, bf16[512,1024]{1,0:T(8,128)(2,1)S(1)}, u32[]{:S(2)}, u32[]{:S(2)}) %collective-permute-start.2) | collective-permute-done | bytes 1048608 | tf_op jit(solution)/shard_map/ppermute | solution.py:14
  304.0 0.0 copy-start
  304.0 1.0 copy-done
  305.0 0.0 all-gather.13.cloned.1.call-update
  305.0 0.0 all-gather.15.cloned.1.call-start
  305.0 81.2 %all-gather.13.cloned.1.call-done = bf16[2048,1024]{1,0:T(8,128)(2,1)} async-done(((bf16[512,1024]{1,0:T(8,128)(2,1)}), bf16[2048,1024]{1,0:T(8,128)(2,1)}) %all-gather.13.cloned.1.call-update) | async-done | bytes 4194320 | tf_op jit(solution)/shard_map/all_gather | solution.py:30
  386.3 5.5 %convolution_convert_fusion = bf16[512,1024]{1,0:T(8,128)(2,1)} fusion(bf16[2048,1024]{1,0:T(8,128)(2,1)} %all-gather.13.cloned.1.call-done, bf16[2048,512]{1,0:T(8,128)(2,1)S(1)} %dynamic-slice_bitcast_fusion, bf16[2048,512]{1,0:T(8,128)(2,1)} %collective-permute-done.1, pred[]{:T(512)S(6)} %eq.9), kind=kOutput, calls=%fused_computation.13 | convolution fusion | flops 2149056512 | bytes 9437185 | tf_op jit(solution)/shard_map/dot_general | solution.py:37
  391.8 0.0 all-gather.15.cloned.1.call-update
  391.8 9.9 %all-gather.15.cloned.1.call-done = bf16[512,2048]{1,0:T(8,128)(2,1)} async-done(((bf16[512,1024]{1,0:T(8,128)(2,1)}), bf16[512,2048]{1,0:T(8,128)(2,1)}) %all-gather.15.cloned.1.call-update) | async-done | bytes 2097168 | tf_op jit(solution)/shard_map/all_gather | solution.py:50
  401.7 7.1 %select_bitcast_fusion = f32[1,512,1024]{2,1,0:T(8,128)} fusion(f32[512,1024]{1,0:T(8,128)} %get-tuple-element.6, f32[512,1024]{1,0:T(8,128)} %fusion.4, bf16[512,2048]{1,0:T(8,128)(2,1)} %all-gather.15.cloned.1.call-done, bf16[1,2048,1024]{2,1,0:T(8,128)(2,1)} %all-gather.19.cloned.1.call-done, pred[]{:T(512)S(6)} %eq.8), kind=kOutput, calls=%fused_computation.8 | convolution fusion | flops 2148532224 | bytes 12582913 | tf_op jit(solution)/shard_map/dot_general | solution.py:51
Async XLA Ops:
  6.5 85.9 %all-gather.19.cloned.1.call-start = ((), (), s32[]{:S(2)}) async-start(), calls=%async_computation.5 | async-start | bytes 5242880 | tf_op jit(solution)/shard_map/all_gather | solution.py:30
  7.3 166.1 %all-gather.17.cloned.1.call-start = ((), (), s32[]{:S(2)}) async-start(), calls=%async_computation.4 | async-start | bytes 5242880 | tf_op jit(solution)/shard_map/all_gather | solution.py:30
  8.0 246.2 %all-gather.9.cloned.1.call-start = ((), (), s32[]{:S(2)}) async-start(), calls=%async_computation | async-start | bytes 5242880 | tf_op jit(solution)/shard_map/all_gather | solution.py:30
  10.8 258.9 %all-gather.11.cloned.1.call-start = ((), (), s32[]{:S(2)}) async-start(), calls=%async_computation.1 | async-start | bytes 3145728 | tf_op jit(solution)/shard_map/all_gather | solution.py:50
  94.2 160.1 %collective-permute-start.1 = (bf16[2048,512]{1,0:T(8,128)(2,1)S(1)}, bf16[2048,512]{1,0:T(8,128)(2,1)}, u32[]{:S(2)}, u32[]{:S(2)}) collective-permute-start(bf16[2048,512]{1,0:T(8,128)(2,1)S(1)} %dynamic-slice_bitcast_fusion), channel_id=1, source_target_pairs={{0,1},{1,0},{2,3},{3,2},{4,5},{5,4},{6,7},{7,6},{8,9},{9,8},{10,11... | collective-permute-start | bytes 6291464 | tf_op jit(solution)/shard_map/ppermute | solution.py:8
  176.4 83.5 %collective-permute-start = (bf16[2048,512]{1,0:T(8,128)(2,1)}, bf16[2048,512]{1,0:T(8,128)(2,1)}, u32[]{:S(2)}, u32[]{:S(2)}) collective-permute-start(bf16[2048,512]{1,0:T(8,128)(2,1)} %dynamic-slice_bitcast_fusion.1), channel_id=1, source_target_pairs={{0,1},{1,0},{2,3},{3,2},{4,5},{5,4},{6,7},{7,6},{8,9},{9,8},{10,11... | collective-permute-start | bytes 6291464 | tf_op jit(solution)/shard_map/ppermute | solution.py:8
  259.8 126.5 %all-gather.13.cloned.1.call-start = ((), (), s32[]{:S(2)}) async-start(), calls=%async_computation.2 | async-start | bytes 5242880 | tf_op jit(solution)/shard_map/all_gather | solution.py:30
  276.8 27.2 %collective-permute-start.2 = (bf16[512,1024]{1,0:T(8,128)(2,1)S(1)}, bf16[512,1024]{1,0:T(8,128)(2,1)S(1)}, u32[]{:S(2)}, u32[]{:S(2)}) collective-permute-start(bf16[512,1024]{1,0:T(8,128)(2,1)S(1)} %get-tuple-element.5), channel_id=1, source_target_pairs={{8,0},{9,1},{10,2},{11,3},{12,4},{13,5},{14,6},{15,7},{24,16},{25,... | collective-permute-start | bytes 3145736 | tf_op jit(solution)/shard_map/ppermute | solution.py:14
  304.0 1.0 copy-start
  305.0 96.7 %all-gather.15.cloned.1.call-start = ((), (), s32[]{:S(2)}) async-start(), calls=%async_computation.3 | async-start | bytes 3145728 | tf_op jit(solution)/shard_map/all_gather | solution.py:50
Sparse Core Ops, SparseCore 0:
  8.9 83.4 all-gather.18
  94.0 79.2 all-gather.16
  174.9 79.2 all-gather.8
  259.9 9.7 all-gather.10
  305.1 81.1 all-gather.12
  391.9 9.7 all-gather.14
where the time goes:
time: 416 us
  waiting for transfers between devices  360 us (87%)
  matrix products  31.9 us (8%)
  between operations  13.5 us (3%)
  local copies, waits for them, and re-layouts  5.75 us (1%)
    all_gather x4, waiting for transfers between devices, gather(): return lax.all_gather(tile, 'row', axis=0, tiled=True)  320 us
    ppermute x1, waiting for transfers between devices, passed_along(): lax.ppermute(value, axis, [(source, source + steps) for source in range(f...  25.9 us
    dot_general x3, matrix products, cross(): lax.dot_general(left, full, (((0,), (0,)), ((), ())), preferred_element_t...  17.7 us
    dot_general x2, matrix products, local(): jnp.dot(whole, factor, preferred_element_type=jnp.float32)  14.2 us
    all_gather x2, waiting for transfers between devices, local(): whole = lax.all_gather(half, 'col', axis=1, tiled=True)  13.1 us
  transfers between devices with their start and end apart: 9, of which 7 were waited for; matrix products, arithmetic and copies ran while one was open for 5% of the time, Pallas kernels for 0%

commit v1 on v0

--- a/solution.py
+++ b/solution.py
@@ -2,6 +2,22 @@
 import jax.numpy as jnp
 from jax import lax
 from jax.sharding import PartitionSpec as P
+
+
+def collect(x, axis, dim):
+    ways, here, step = (lax.axis_size(axis), lax.axis_index(axis), x.shape[dim])
+    dims = [n * ways if d == dim else n for d, n in enumerate(x.shape)]
+    full = lax.dynamic_update_slice_in_dim(jnp.zeros(dims, x.dtype), x, here * step, axis=dim)
+    going_up = going_down = x
+    for far in range(1, ways // 2 + 1):
+        going_up = lax.ppermute(going_up, axis, [(d, (d + 1) % ways) for d in range(ways)])
+        full = lax.dynamic_update_slice_in_dim(full, going_up, (here - far) % ways * step, axis=dim)
+        if 2 * far < ways:
+            going_down = lax.ppermute(going_down, axis, [(d, (d - 1) % ways) for d in range(ways)])
+            full = lax.dynamic_update_slice_in_dim(
+                full, going_down, (here + far) % ways * step, axis=dim
+            )
+    return full
 
 
 def partner(shard, axis, stride):
@@ -27,7 +43,7 @@
     owns_panel = col_index == row_index // per_column
 
     def gather(tile):
-        return lax.all_gather(tile, "row", axis=0, tiled=True)
+        return collect(tile, "row", 0)
 
     def left_of(full):
         mine = lax.dynamic_slice_in_dim(full, offset, tile_rows, 1)

time: 416 us -> 368 us (0.88)
  waiting for transfers between devices: 360 us -> 213 us
  starting transfers between devices: 1.56 us -> 79.8 us
  local copies, waits for them, and re-layouts: 5.75 us -> 30 us
    all_gather x4 -> x0, waiting for transfers between devices: 320 us -> none  [gather(): return lax.all_gather(tile, 'row', axis=0, tiled=True)]
    ppermute x0 -> x12, waiting for transfers between devices: none -> 172 us  [the longest x8 151 us: collect(): lax.ppermute(going_up, axis, [(d, (d + 1) % ways) for d in range(ways)])]
    ppermute x0 -> x12, starting transfers between devices: none -> 78.4 us  [the longest x8 72 us: collect(): lax.ppermute(going_up, axis, [(d, (d + 1) % ways) for d in range(ways)])]
    dynamic_update_slice x0 -> x15, local copies, waits for them, and re-layouts: none -> 20.6 us  [the longest x8 12.1 us: collect(): lax.dynamic_update_slice_in_dim(full, going_up, (here - far) % ways * ste...]
    another operation x0 -> x4, local copies, waits for them, and re-layouts: none -> 6.1 us
  transfers between devices with their start and end apart: 9 -> 17, of which waited for: 7 -> 12; matrix products, arithmetic and copies ran while one was open for 5% -> 12% of each run, Pallas kernels for 0% -> 0%
where the time goes in v1:
time: 368 us; the launch traced here: 367 us
  waiting for transfers between devices  213 us (58%)
  starting transfers between devices  79.8 us (22%)
  local copies, waits for them, and re-layouts  30 us (8%)
  matrix products  29.7 us (8%)
  between operations  13.6 us (4%)
    ppermute x8, waiting for transfers between devices, collect(): lax.ppermute(going_up, axis, [(d, (d + 1) % ways) for d in range(ways)])  151 us
    ppermute x8, starting transfers between devices, collect(): lax.ppermute(going_up, axis, [(d, (d + 1) % ways) for d in range(ways)])  72 us
    ppermute x1, waiting for transfers between devices, passed_along(): lax.ppermute(value, axis, [(source, source + steps) for source in range(f...  25.9 us
    ppermute x4, waiting for transfers between devices, collect(): lax.ppermute(going_down, axis, [(d, (d - 1) % ways) for d in range(ways)])  20.8 us
    dot_general x3, matrix products, cross(): lax.dot_general(left, full, (((0,), (0,)), ((), ())), preferred_element_t...  15.5 us
    all_gather x2, waiting for transfers between devices, local(): whole = lax.all_gather(half, 'col', axis=1, tiled=True)  14.7 us
    dot_general x2, matrix products, local(): jnp.dot(whole, factor, preferred_element_type=jnp.float32)  14.2 us
    dynamic_update_slice x8, local copies, waits for them, and re-layouts, collect(): lax.dynamic_update_slice_in_dim(full, going_up, (here - far) % ways * ste...  12.1 us
  transfers between devices with their start and end apart: 17, of which 12 were waited for; matrix products, arithmetic and copies ran while one was open for 12% of the time, Pallas kernels for 0%

profile of v1, /device:TPU:0, one launch (start us, length us, event | category | flops | bytes accessed | tf_op | source)
XLA Modules:
  0.0 367.3 jit_solution(16026790897290025642)
XLA Ops:
  6.5 0.0 all-gather.3.cloned.1.call-start
  6.5 3.0 collective-permute-start.4
  9.6 2.0 collective-permute-start.5
  11.6 24.3 %collective-permute-done.4 = bf16[512,1024]{1,0:T(8,128)(2,1)} collective-permute-done((bf16[512,1024]{1,0:T(8,128)(2,1)}, bf16[512,1024]{1,0:T(8,128)(2,1)}, u32[]{:S(2)}, u32[]{:S(2)}) %collective-permute-start.4) | collective-permute-done | bytes 1048608 | tf_op jit(solution)/shard_map/ppermute | solution.py:13
  35.9 0.0 collective-permute-start.6
  35.9 21.8 %collective-permute-start = (bf16[512,1024]{1,0:T(8,128)(2,1)}, bf16[512,1024]{1,0:T(8,128)(2,1)}, u32[]{:S(2)}, u32[]{:S(2)}) collective-permute-start(bf16[512,1024]{1,0:T(8,128)(2,1)} %bitcast), channel_id=1, source_target_pairs={{0,2},{2,4},{4,6},{6,0},{1,3},{3,5},{5,7},{7,1},{8,10},{10,12},{12... | collective-permute-start | bytes 3145736 | tf_op jit(solution)/shard_map/ppermute | solution.py:13
  57.7 2.5 broadcast.8.clone.1
  60.2 0.0 copy-done.1
  60.2 1.4 constant_dynamic-update-slice_fusion.7
  61.6 1.6 collective-permute-start.8
  63.2 0.5 broadcast.8.clone.2
  63.8 0.1 constant_dynamic-update-slice_fusion.11
  63.9 1.3 constant_dynamic-update-slice_fusion.10
  65.2 0.0 collective-permute-done.5
  65.2 1.3 constant_dynamic-update-slice_fusion.9
  66.6 16.1 %collective-permute-done.6 = bf16[512,1024]{1,0:T(8,128)(2,1)} collective-permute-done((bf16[512,1024]{1,0:T(8,128)(2,1)}, bf16[512,1024]{1,0:T(8,128)(2,1)}, u32[]{:S(2)}, u32[]{:S(2)}) %collective-permute-start.6) | collective-permute-done | bytes 1048608 | tf_op jit(solution)/shard_map/ppermute | solution.py:13
  82.7 1.3 constant_dynamic-update-slice_fusion.8
  84.0 0.2 constant_dynamic-slice_fusion
  84.3 0.1 collective-permute-start.7
  84.4 2.1 collective-permute-start.1
  86.5 0.3 collective-permute-start.9
  86.8 18.6 %collective-permute-done = bf16[512,1024]{1,0:T(8,128)(2,1)} collective-permute-done((bf16[512,1024]{1,0:T(8,128)(2,1)}, bf16[512,1024]{1,0:T(8,128)(2,1)}, u32[]{:S(2)}, u32[]{:S(2)}) %collective-permute-start) | collective-permute-done | bytes 1048608 | tf_op jit(solution)/shard_map/ppermute | solution.py:13
  105.4 0.0 collective-permute-start.2
  105.4 22.4 %collective-permute-done.8 = bf16[512,1024]{1,0:T(8,128)(2,1)} collective-permute-done((bf16[512,1024]{1,0:T(8,128)(2,1)S(1)}, bf16[512,1024]{1,0:T(8,128)(2,1)}, u32[]{:S(2)}, u32[]{:S(2)}) %collective-permute-start.8) | collective-permute-done | bytes 1048608 | tf_op jit(solution)/shard_map/ppermute | solution.py:13
  127.7 43.7 %collective-permute-start.10 = (bf16[512,1024]{1,0:T(8,128)(2,1)}, bf16[512,1024]{1,0:T(8,128)(2,1)}, u32[]{:S(2)}, u32[]{:S(2)}) collective-permute-start(bf16[512,1024]{1,0:T(8,128)(2,1)} %collective-permute-done.8), channel_id=1, source_target_pairs={{0,2},{2,4},{4,6},{6,0},{1,3},{3,5},{5,7},{7,1},{8,10},{10,12},{12... | collective-permute-start | bytes 3145736 | tf_op jit(solution)/shard_map/ppermute | solution.py:13
  171.4 2.5 broadcast.8.clone
  174.0 2.3 constant_dynamic-update-slice_fusion.15
  176.3 2.4 constant_dynamic-update-slice_fusion.14
  178.6 2.3 constant_dynamic-update-slice_fusion.6
  180.9 0.0 collective-permute-done.1
  180.9 2.3 constant_dynamic-update-slice_fusion.13
  183.2 0.0 collective-permute-done.9
  183.2 2.3 constant_dynamic-update-slice_fusion.5
  185.5 9.6 %collective-permute-done.2 = bf16[512,1024]{1,0:T(8,128)(2,1)} collective-permute-done((bf16[512,1024]{1,0:T(8,128)(2,1)}, bf16[512,1024]{1,0:T(8,128)(2,1)}, u32[]{:S(2)}, u32[]{:S(2)}) %collective-permute-start.2) | collective-permute-done | bytes 1048608 | tf_op jit(solution)/shard_map/ppermute | solution.py:13
  195.1 2.3 constant_dynamic-update-slice_fusion.12
  197.4 3.0 constant_dynamic-slice_fusion.1
  200.4 0.0 collective-permute-start.3
  200.4 14.5 %collective-permute-done.10 = bf16[512,1024]{1,0:T(8,128)(2,1)} collective-permute-done((bf16[512,1024]{1,0:T(8,128)(2,1)}, bf16[512,1024]{1,0:T(8,128)(2,1)}, u32[]{:S(2)}, u32[]{:S(2)}) %collective-permute-start.10) | collective-permute-done | bytes 1048608 | tf_op jit(solution)/shard_map/ppermute | solution.py:13
  215.0 2.3 constant_dynamic-update-slice_fusion.4
  217.2 0.0 collective-permute-done.7
  217.2 5.6 %convolution_convert_fusion.1 = bf16[512,1024]{1,0:T(8,128)(2,1)} fusion(bf16[2048,1024]{1,0:T(8,128)(2,1)} %constant_dynamic-update-slice_fusion.4, bf16[2048,512]{1,0:T(8,128)(2,1)S(1)} %constant_dynamic-slice_fusion, bf16[2048,512]{1,0:T(8,128)(2,1)} %collective-permute-done.7, pred[]{:T(512)S(6)} %eq.21), kind=kOutput, calls=%fused_computation.7 | convolution fusion | flops 2149056512 | bytes 9437185 | tf_op jit(solution)/shard_map/dot_general | solution.py:53
  222.8 0.0 all-gather.3.cloned.1.call-update
  222.8 0.0 all-gather.5.cloned.1.call-start
  222.9 0.0 collective-permute-done.3
  222.9 6.6 %fusion = f32[512,1024]{1,0:T(8,128)} fusion(bf16[2048,1024]{1,0:T(8,128)(2,1)} %constant_dynamic-update-slice_fusion.12, bf16[2048,512]{1,0:T(8,128)(2,1)} %constant_dynamic-slice_fusion.1, bf16[2048,512]{1,0:T(8,128)(2,1)} %collective-permute-done.3, pred[]{:T(512)S(6)} %eq.21), kind=kOutput, calls=%fused_computation.1 | convolution fusion | flops 2148532224 | bytes 10485761 | tf_op jit(solution)/shard_map/dot_general | solution.py:53
  229.5 4.0 %all-gather.3.cloned.1.call-done = bf16[512,2048]{1,0:T(8,128)(2,1)} async-done(((bf16[512,1024]{1,0:T(8,128)(2,1)}), bf16[512,2048]{1,0:T(8,128)(2,1)}) %all-gather.3.cloned.1.call-update) | async-done | bytes 2097168 | tf_op jit(solution)/shard_map/all_gather | solution.py:66
  233.4 7.1 %fusion.3 = (bf16[512,1024]{1,0:T(8,128)(2,1)S(1)}, f32[512,1024]{1,0:T(8,128)}) fusion(f32[512,1024]{1,0:T(8,128)} %fusion, bf16[512,2048]{1,0:T(8,128)(2,1)} %all-gather.3.cloned.1.call-done, bf16[2048,1024]{1,0:T(8,128)(2,1)} %copy-done), kind=kOutput, calls=%fused_computation.26 | convolution fusion | flops 2148532224 | bytes 11534336 | tf_op jit(solution)/shard_map/dot_general | solution.py:67
  240.6 1.3 collective-permute-start.11
  241.9 25.9 %collective-permute-done.11 = bf16[512,1024]{1,0:T(8,128)(2,1)S(1)} collective-permute-done((bf16[512,1024]{1,0:T(8,128)(2,1)S(1)}, bf16[512,1024]{1,0:T(8,128)(2,1)S(1)}, u32[]{:S(2)}, u32[]{:S(2)}) %collective-permute-start.11) | collective-permute-done | bytes 1048608 | tf_op jit(solution)/shard_map/ppermute | solution.py:30
  267.7 1.8 collective-permute-start.12
  269.6 2.0 collective-permute-start.13
  271.6 24.1 %collective-permute-done.12 = bf16[512,1024]{1,0:T(8,128)(2,1)S(1)} collective-permute-done((bf16[512,1024]{1,0:T(8,128)(2,1)S(1)}, bf16[512,1024]{1,0:T(8,128)(2,1)S(1)}, u32[]{:S(2)}, u32[]{:S(2)}) %collective-permute-start.12) | collective-permute-done | bytes 1048608 | tf_op jit(solution)/shard_map/ppermute | solution.py:13
  295.6 0.0 collective-permute-start.14
  295.7 0.5 broadcast.8
  296.2 0.1 constant_dynamic-update-slice_fusion.3
  296.3 0.1 constant_dynamic-update-slice_fusion.2
  296.4 20.8 %collective-permute-done.13 = bf16[512,1024]{1,0:T(8,128)(2,1)S(1)} collective-permute-done((bf16[512,1024]{1,0:T(8,128)(2,1)S(1)}, bf16[512,1024]{1,0:T(8,128)(2,1)S(1)}, u32[]{:S(2)}, u32[]{:S(2)}) %collective-permute-start.13) | collective-permute-done | bytes 1048608 | tf_op jit(solution)/shard_map/ppermute | solution.py:16
  317.3 0.1 constant_dynamic-update-slice_fusion.1
  317.4 21.8 %collective-permute-done.14 = bf16[512,1024]{1,0:T(8,128)(2,1)S(1)} collective-permute-done((bf16[512,1024]{1,0:T(8,128)(2,1)S(1)}, bf16[512,1024]{1,0:T(8,128)(2,1)S(1)}, u32[]{:S(2)}, u32[]{:S(2)}) %collective-permute-start.14) | collective-permute-done | bytes 1048608 | tf_op jit(solution)/shard_map/ppermute | solution.py:13
  339.2 0.1 constant_dynamic-update-slice_fusion
  339.3 3.3 convolution_convert_fusion
  342.7 0.0 all-gather.5.cloned.1.call-update
  342.7 10.7 %all-gather.5.cloned.1.call-done = bf16[512,2048]{1,0:T(8,128)(2,1)} async-done(((bf16[512,1024]{1,0:T(8,128)(2,1)}), bf16[512,2048]{1,0:T(8,128)(2,1)}) %all-gather.5.cloned.1.call-update) | async-done | bytes 2097168 | tf_op jit(solution)/shard_map/all_gather | solution.py:66
  353.4 7.1 %select_bitcast_fusion = f32[1,512,1024]{2,1,0:T(8,128)} fusion(f32[512,1024]{1,0:T(8,128)} %get-tuple-element.8, f32[512,1024]{1,0:T(8,128)} %fusion, bf16[512,2048]{1,0:T(8,128)(2,1)} %all-gather.5.cloned.1.call-done, bf16[2048,1024]{1,0:T(8,128)(2,1)} %copy-done, pred[]{:T(512)S(6)} %eq.20), kind=kOutput, calls=%fused_computation | convolution fusion | flops 2148532224 | bytes 12582913 | tf_op jit(solution)/shard_map/dot_general | solution.py:67
  (5 shorter events, 0.0 us)
Async XLA Ops:
  6.5 53.7 %copy-start.1 = (f32[512,1024]{1,0:T(8,128)S(1)}, f32[512,1024]{1,0:T(8,128)}, u32[]{:S(2)}) copy-start(f32[512,1024]{1,0:T(8,128)} %param.5) | copy-start | bytes 6291460
  6.5 226.9 %all-gather.3.cloned.1.call-start = ((), (), s32[]{:S(2)}) async-start(), calls=%async_computation | async-start | bytes 3145728 | tf_op jit(solution)/shard_map/all_gather | solution.py:66
  6.5 29.4 %collective-permute-start.4 = (bf16[512,1024]{1,0:T(8,128)(2,1)}, bf16[512,1024]{1,0:T(8,128)(2,1)}, u32[]{:S(2)}, u32[]{:S(2)}) collective-permute-start(bf16[512,1024]{1,0:T(8,128)(2,1)} %bitcast.13), channel_id=1, source_target_pairs={{0,2},{2,4},{4,6},{6,0},{1,3},{3,5},{5,7},{7,1},{8,10},{10,12},{12... | collective-permute-start | bytes 3145736 | tf_op jit(solution)/shard_map/ppermute | solution.py:13
  9.6 55.7 %collective-permute-start.5 = (bf16[512,1024]{1,0:T(8,128)(2,1)}, bf16[512,1024]{1,0:T(8,128)(2,1)}, u32[]{:S(2)}, u32[]{:S(2)}) collective-permute-start(bf16[512,1024]{1,0:T(8,128)(2,1)} %bitcast.14), channel_id=1, source_target_pairs={{0,6},{2,0},{4,2},{6,4},{1,7},{3,1},{5,3},{7,5},{8,14},{10,8},{12,... | collective-permute-start | bytes 3145736 | tf_op jit(solution)/shard_map/ppermute | solution.py:16
  35.9 46.8 %collective-permute-start.6 = (bf16[512,1024]{1,0:T(8,128)(2,1)}, bf16[512,1024]{1,0:T(8,128)(2,1)}, u32[]{:S(2)}, u32[]{:S(2)}) collective-permute-start(bf16[512,1024]{1,0:T(8,128)(2,1)} %collective-permute-done.4), channel_id=1, source_target_pairs={{0,2},{2,4},{4,6},{6,0},{1,3},{3,5},{5,7},{7,1},{8,10},{10,12},{12... | collective-permute-start | bytes 3145736 | tf_op jit(solution)/shard_map/ppermute | solution.py:13
  35.9 69.4 %collective-permute-start = (bf16[512,1024]{1,0:T(8,128)(2,1)}, bf16[512,1024]{1,0:T(8,128)(2,1)}, u32[]{:S(2)}, u32[]{:S(2)}) collective-permute-start(bf16[512,1024]{1,0:T(8,128)(2,1)} %bitcast), channel_id=1, source_target_pairs={{0,2},{2,4},{4,6},{6,0},{1,3},{3,5},{5,7},{7,1},{8,10},{10,12},{12... | collective-permute-start | bytes 3145736 | tf_op jit(solution)/shard_map/ppermute | solution.py:13
  61.6 2.1 copy-start.2
  61.6 66.1 %collective-permute-start.8 = (bf16[512,1024]{1,0:T(8,128)(2,1)S(1)}, bf16[512,1024]{1,0:T(8,128)(2,1)}, u32[]{:S(2)}, u32[]{:S(2)}) collective-permute-start(bf16[512,1024]{1,0:T(8,128)(2,1)S(1)} %get-tuple-element.6), channel_id=1, source_target_pairs={{0,2},{2,4},{4,6},{6,0},{1,3},{3,5},{5,7},{7,1},{8,10},{10,12},{12... | collective-permute-start | bytes 3145736 | tf_op jit(solution)/shard_map/ppermute | solution.py:13
  84.0 90.0 %copy-start = (bf16[2048,1024]{1,0:T(8,128)(2,1)}, bf16[2048,1024]{1,0:T(8,128)(2,1)S(1)}, u32[]{:S(2)}) copy-start(bf16[2048,1024]{1,0:T(8,128)(2,1)S(1)} %constant_dynamic-update-slice_fusion.8) | copy-start | bytes 12582916
  84.3 132.9 %collective-permute-start.7 = (bf16[2048,512]{1,0:T(8,128)(2,1)S(1)}, bf16[2048,512]{1,0:T(8,128)(2,1)}, u32[]{:S(2)}, u32[]{:S(2)}) collective-permute-start(bf16[2048,512]{1,0:T(8,128)(2,1)S(1)} %constant_dynamic-slice_fusion), channel_id=1, source_target_pairs={{0,1},{1,0},{2,3},{3,2},{4,5},{5,4},{6,7},{7,6},{8,9},{9,8},{10,11... | collective-permute-start | bytes 6291464 | tf_op jit(solution)/shard_map/ppermute | solution.py:24
  84.4 96.6 %collective-permute-start.1 = (bf16[512,1024]{1,0:T(8,128)(2,1)}, bf16[512,1024]{1,0:T(8,128)(2,1)}, u32[]{:S(2)}, u32[]{:S(2)}) collective-permute-start(bf16[512,1024]{1,0:T(8,128)(2,1)} %bitcast), channel_id=1, source_target_pairs={{0,6},{2,0},{4,2},{6,4},{1,7},{3,1},{5,3},{7,5},{8,14},{10,8},{12,... | collective-permute-start | bytes 3145736 | tf_op jit(solution)/shard_map/ppermute | solution.py:16
  86.5 96.8 %collective-permute-start.9 = (bf16[512,1024]{1,0:T(8,128)(2,1)S(1)}, bf16[512,1024]{1,0:T(8,128)(2,1)}, u32[]{:S(2)}, u32[]{:S(2)}) collective-permute-start(bf16[512,1024]{1,0:T(8,128)(2,1)S(1)} %get-tuple-element.6), channel_id=1, source_target_pairs={{0,6},{2,0},{4,2},{6,4},{1,7},{3,1},{5,3},{7,5},{8,14},{10,8},{12,... | collective-permute-start | bytes 3145736 | tf_op jit(solution)/shard_map/ppermute | solution.py:16
  105.4 89.8 %collective-permute-start.2 = (bf16[512,1024]{1,0:T(8,128)(2,1)}, bf16[512,1024]{1,0:T(8,128)(2,1)}, u32[]{:S(2)}, u32[]{:S(2)}) collective-permute-start(bf16[512,1024]{1,0:T(8,128)(2,1)} %collective-permute-done), channel_id=1, source_target_pairs={{0,2},{2,4},{4,6},{6,0},{1,3},{3,5},{5,7},{7,1},{8,10},{10,12},{12... | collective-permute-start | bytes 3145736 | tf_op jit(solution)/shard_map/ppermute | solution.py:13
  127.7 87.2 %collective-permute-start.10 = (bf16[512,1024]{1,0:T(8,128)(2,1)}, bf16[512,1024]{1,0:T(8,128)(2,1)}, u32[]{:S(2)}, u32[]{:S(2)}) collective-permute-start(bf16[512,1024]{1,0:T(8,128)(2,1)} %collective-permute-done.8), channel_id=1, source_target_pairs={{0,2},{2,4},{4,6},{6,0},{1,3},{3,5},{5,7},{7,1},{8,10},{10,12},{12... | collective-permute-start | bytes 3145736 | tf_op jit(solution)/shard_map/ppermute | solution.py:13
  200.4 22.4 %collective-permute-start.3 = (bf16[2048,512]{1,0:T(8,128)(2,1)}, bf16[2048,512]{1,0:T(8,128)(2,1)}, u32[]{:S(2)}, u32[]{:S(2)}) collective-permute-start(bf16[2048,512]{1,0:T(8,128)(2,1)} %constant_dynamic-slice_fusion.1), channel_id=1, source_target_pairs={{0,1},{1,0},{2,3},{3,2},{4,5},{5,4},{6,7},{7,6},{8,9},{9,8},{10,11... | collective-permute-start | bytes 6291464 | tf_op jit(solution)/shard_map/ppermute | solution.py:24
  222.8 130.6 %all-gather.5.cloned.1.call-start = ((), (), s32[]{:S(2)}) async-start(), calls=%async_computation.1 | async-start | bytes 3145728 | tf_op jit(solution)/shard_map/all_gather | solution.py:66
  240.6 27.2 %collective-permute-start.11 = (bf16[512,1024]{1,0:T(8,128)(2,1)S(1)}, bf16[512,1024]{1,0:T(8,128)(2,1)S(1)}, u32[]{:S(2)}, u32[]{:S(2)}) collective-permute-start(bf16[512,1024]{1,0:T(8,128)(2,1)S(1)} %get-tuple-element.7), channel_id=1, source_target_pairs={{8,0},{9,1},{10,2},{11,3},{12,4},{13,5},{14,6},{15,7},{24,16},{25,... | collective-permute-start | bytes 3145736 | tf_op jit(solution)/shard_map/ppermute | solution.py:30
  267.7 27.9 %collective-permute-start.12 = (bf16[512,1024]{1,0:T(8,128)(2,1)S(1)}, bf16[512,1024]{1,0:T(8,128)(2,1)S(1)}, u32[]{:S(2)}, u32[]{:S(2)}) collective-permute-start(bf16[512,1024]{1,0:T(8,128)(2,1)S(1)} %collective-permute-done.11), channel_id=1, source_target_pairs={{0,2},{2,4},{4,6},{6,0},{1,3},{3,5},{5,7},{7,1},{8,10},{10,12},{12... | collective-permute-start | bytes 3145736 | tf_op jit(solution)/shard_map/ppermute | solution.py:13
  269.6 47.7 %collective-permute-start.13 = (bf16[512,1024]{1,0:T(8,128)(2,1)S(1)}, bf16[512,1024]{1,0:T(8,128)(2,1)S(1)}, u32[]{:S(2)}, u32[]{:S(2)}) collective-permute-start(bf16[512,1024]{1,0:T(8,128)(2,1)S(1)} %collective-permute-done.11), channel_id=1, source_target_pairs={{0,6},{2,0},{4,2},{6,4},{1,7},{3,1},{5,3},{7,5},{8,14},{10,8},{12,... | collective-permute-start | bytes 3145736 | tf_op jit(solution)/shard_map/ppermute | solution.py:16
  295.6 43.6 %collective-permute-start.14 = (bf16[512,1024]{1,0:T(8,128)(2,1)S(1)}, bf16[512,1024]{1,0:T(8,128)(2,1)S(1)}, u32[]{:S(2)}, u32[]{:S(2)}) collective-permute-start(bf16[512,1024]{1,0:T(8,128)(2,1)S(1)} %collective-permute-done.12), channel_id=1, source_target_pairs={{0,2},{2,4},{4,6},{6,0},{1,3},{3,5},{5,7},{7,1},{8,10},{10,12},{12... | collective-permute-start | bytes 3145736 | tf_op jit(solution)/shard_map/ppermute | solution.py:13
Sparse Core Ops, SparseCore 0:
  222.9 10.4 all-gather.2
  342.8 10.5 all-gather.4
